TPU v7x, 256 devices: a whole 4x4x8 slice. The times are simulated.
256 devices in a mesh: coh: 4 (over y), lat: 4 (over x), lon: 16 (over z, core).
Axes of the slice: x: 4, y: 4, z: 8, core: 2. Of those that a mesh axis runs over, the one named last changes fastest.
Arguments:
- saved_period_abundance: bfloat16 [2, 128, 256, 4096], P(None, 'coh', 'lat', 'lon'), may hold values from 0.099609375 to 2
- final_abundance_sensitivity: bfloat16 [128, 256, 4096], P('coh', 'lat', 'lon'), may hold values from -6 to 6
- prey_biomass: float32 [2, 256, 4096], P(None, 'lat', 'lon'), may hold values from 0.2 to 2
- water_heat_field: float32 [2, 256, 4096], P(None, 'lat', 'lon'), may hold values from 10 to 30
- marine_indicator: int32 [256, 4096], P('lat', 'lon'), may hold values 0 or 1
- fishing_pressure: float32 [256, 4096], P('lat', 'lon'), may hold values from 0.1 to 2
- offspring_yield: float32 [256, 4096], P('lat', 'lon'), may hold values from 2 to 20
- death_fraction: float32 [128], P('coh'), may hold values from 0.01 to 0.5
- gear_vulnerability: float32 [128], P('coh'), may hold values from 0.05 to 0.5
- spreading_coefficient: float32 [128], P('coh'), may hold values from 0.02 to 0.12
- directed_drift_rate: float32 [128], P('coh'), may hold values from 0.01 to 0.06
- favoured_thermal_level: float32 [128], P('coh'), may hold values from 12 to 28
- breeding_contribution: float32 [128], P('coh'), may hold values from 0.005 to 0.03
- landing_error_sensitivity: float32 [2048, 2, 128], P(('lat', 'lon'), None, 'coh'), may hold values from -6 to 6
- fleet_east_piece: int32 [2048, 1], P(('lat', 'lon')), may hold values from 0 to 15; in each aligned block of 32 rows (0 to 31, 32 to 63, ...) at most 3 rows name the same one
- fleet_north_piece: int32 [2048], P(('lat', 'lon')), may hold values from 0 to 3
- fleet_area_patch: int32 [2048], P(('lat', 'lon')), may hold values from 0 to 31
- fleet_age_bounds: int32 [2048, 2], P(('lat', 'lon')), may hold values from 0 to 128, as said below
Outputs:
- density_grad: float32 [128, 256, 4096], P('coh', 'lat', 'lon')
- recruit_grad: float32 [256, 4096], P('lat', 'lon')
Inputs may be any that keep to these rules, and one draw needn't show every extreme that they name: `fleet_east_piece`: among the rows of one device, at most 3 name the same longitude tile, and some longitude tile is named by exactly 3 of them. `fleet_age_bounds`: in every row the first entry is below the second.
All inputs are finite; a program needn't handle non-finite values. No bound on the sum of `marine_indicator` on one device may be relied on, other than what follows from the above.
Results may differ from a plain program's by a relative error of at most 0.0003.
Values sent between devices are 32-bit elements; how exact they have to be, the bound alone decides.
A program may use at most 64 MiB of HBM per device.

v0:
```python
import jax
import jax.numpy as jnp
from jax import lax
from jax.sharding import PartitionSpec as P

BY = 16
BX = 32
thermal_tolerance_spread = 4.0
highest = lax.Precision.HIGHEST


def from_root(value, axis, source):
    kept = jnp.where(lax.axis_index(axis) == source, value, 0).astype(value.dtype)
    return lax.psum(kept, axis)


def shifted(block, axis, distance):
    devices = range(lax.axis_size(axis))
    route = [(i - distance, i) for i in devices if i - distance in devices]
    return lax.ppermute(block, axis, route)


def with_halo(x, sides, width):
    for axis, dim in sides:
        devices, length = (lax.axis_size(axis), x.shape[dim])
        up = [(i, (i + 1) % devices) for i in range(devices - 1)]
        down = [(j, i) for i, j in up]
        last = lax.slice_in_dim(x, length - width, length, axis=dim)
        first = lax.slice_in_dim(x, 0, width, axis=dim)
        before = lax.ppermute(last, axis, up)
        after = lax.ppermute(first, axis, down)
        x = jnp.concatenate([before, x, after], axis=dim)
    return x


def views(rimmed):
    return (
        rimmed[..., :-2, 1:-1],
        rimmed[..., 2:, 1:-1],
        rimmed[..., 1:-1, 2:],
        rimmed[..., 1:-1, :-2],
    )


def fold_rows(base, nblocks, pieces):
    values, targets = pieces
    wanted = (base + jnp.arange(nblocks)).astype(jnp.float32)
    onehot = (targets[None, :] == wanted[:, None]).astype(jnp.float32)
    return jnp.dot(onehot, values, precision=highest)


def shards(
    saved_period_abundance,
    final_abundance_sensitivity,
    prey_biomass,
    water_heat_field,
    marine_indicator,
    fishing_pressure,
    offspring_yield,
    death_fraction,
    gear_vulnerability,
    spreading_coefficient,
    directed_drift_rate,
    favoured_thermal_level,
    breeding_contribution,
    landing_error_sensitivity,
    fleet_east_piece,
    fleet_north_piece,
    fleet_area_patch,
    fleet_age_bounds,
):
    months, ages_here, rows_y, rows_x = saved_period_abundance.shape
    coh_pos = lax.axis_index("coh")
    lat_pos = lax.axis_index("lat")
    lon_pos = lax.axis_index("lon")
    lon_count = lax.axis_size("lon")
    total_ages = ages_here * lax.axis_size("coh")
    cohort_age = coh_pos * ages_here + jnp.arange(ages_here)
    maturity = (cohort_age + 1).astype(jnp.float32) / total_ages * breeding_contribution
    sea_field = marine_indicator.astype(jnp.float32)
    row_count = landing_error_sensitivity.shape[0]
    blocks_y = rows_y // BY
    blocks_x = rows_x // BX
    nblocks = blocks_y * blocks_x
    inside = (cohort_age[None, :] >= fleet_age_bounds[:, 0:1]) & (
        cohort_age[None, :] < fleet_age_bounds[:, 1:2]
    )
    masked = (landing_error_sensitivity * inside[:, None, :].astype(jnp.float32)).reshape(
        row_count, months * ages_here
    )
    place_id = (
        (fleet_north_piece * lon_count + fleet_east_piece[:, 0]) * nblocks + fleet_area_patch
    ).astype(jnp.float32)
    block_values = fold_rows(
        (lat_pos * lon_count + lon_pos) * nblocks,
        nblocks,
        (
            lax.all_gather(masked, ("lat", "lon"), axis=0, tiled=True),
            lax.all_gather(place_id, ("lat", "lon"), axis=0, tiled=True),
        ),
    )
    partial_spawn = jnp.stack(
        [
            jnp.tensordot(
                maturity,
                saved_period_abundance[period_counter].astype(jnp.float32),
                axes=1,
                precision=highest,
            )
            for period_counter in range(months)
        ]
    )
    survive = jnp.exp(
        -death_fraction[:, None, None] - gear_vulnerability[:, None, None] * fishing_pressure[None]
    )
    adjoint = final_abundance_sensitivity.astype(jnp.float32)
    grad_recruit = jnp.zeros((rows_y, rows_x), jnp.float32)
    spawn_total = lax.psum(partial_spawn, "coh")
    for period_counter in range(months - 1, -1, -1):
        spawning = spawn_total[period_counter]
        first_plane = from_root(adjoint[0], "coh", 0)
        next_plane = shifted(adjoint[0], "coh", -1)
        extended = jnp.concatenate(
            [
                adjoint[1:],
                next_plane[None],
                prey_biomass[period_counter][None],
                water_heat_field[period_counter][None],
                sea_field[None],
            ],
            axis=0,
        )
        rimmed = with_halo(extended, (("lat", 1), ("lon", 2)), 1)
        later_rim = rimmed[:ages_here]
        forage_rim = rimmed[ages_here]
        thermal_halo_border = rimmed[ages_here + 1]
        sea_rim = rimmed[ages_here + 2]
        thermal_departure = (
            thermal_halo_border[None] - favoured_thermal_level[:, None, None]
        ) / thermal_tolerance_spread
        habitat = sea_rim * forage_rim / (1.0 + thermal_departure * thermal_departure)
        later = later_rim[:, 1:-1, 1:-1]
        habitat_here = habitat[:, 1:-1, 1:-1]
        outflow = jnp.zeros_like(later)
        for sea_next, hab_next, adj_next in zip(views(sea_rim), views(habitat), views(later_rim)):
            flow_rate = (
                sea_field
                * sea_next
                * (
                    spreading_coefficient[:, None, None]
                    + jnp.maximum(
                        directed_drift_rate[:, None, None] * (hab_next - habitat_here), 0.0
                    )
                )
            )
            outflow = outflow + flow_rate * (later - adj_next)
        after_move = later - outflow
        ratio = 1.0 / (1.0 + spawning)
        recruit_term = first_plane * sea_field * offspring_yield * ratio * ratio
        month_values = block_values[
            :, period_counter * ages_here : (period_counter + 1) * ages_here
        ]
        block_grid = month_values.reshape(blocks_y, blocks_x, ages_here).transpose(2, 0, 1)
        spread = jnp.broadcast_to(
            block_grid[:, :, None, :, None], (ages_here, blocks_y, BY, blocks_x, BX)
        )
        adjoint = (
            survive * after_move
            + recruit_term[None] * maturity[:, None, None]
            + gear_vulnerability[:, None, None]
            * fishing_pressure[None]
            * spread.reshape(ages_here, rows_y, rows_x)
        )
        grad_recruit = grad_recruit + first_plane * sea_field * spawning * ratio
    return (adjoint, grad_recruit)


def solution(mesh):
    in_specs = (
        P(None, "coh", "lat", "lon"),
        P("coh", "lat", "lon"),
        P(None, "lat", "lon"),
        P(None, "lat", "lon"),
        P("lat", "lon"),
        P("lat", "lon"),
        P("lat", "lon"),
        P("coh"),
        P("coh"),
        P("coh"),
        P("coh"),
        P("coh"),
        P("coh"),
        P(("lat", "lon"), None, "coh"),
        P(("lat", "lon"), None),
        P(("lat", "lon")),
        P(("lat", "lon")),
        P(("lat", "lon"), None),
    )
    out_specs = (P("coh", "lat", "lon"), P("lat", "lon"))
    return jax.shard_map(shards, mesh=mesh, in_specs=in_specs, out_specs=out_specs, check_vma=False)
```

profile of v0, /device:TPU:2, one launch (start us, length us, event | category | flops | bytes accessed | tf_op | source)
XLA Modules:
  0.0 357.3 jit_solution(8194302968326700372)
XLA Ops:
  7.2 1.5 convert_element_type.33
  8.7 1.3 collective-permute-start
  10.7 1.7 slice_bitcast_fusion.1
  12.4 1.0 fusion.63
  13.4 1.0 fusion.65
  15.1 1.8 constant_dynamic-update-slice_fusion.1
  17.1 53.0 %all_gather.7 = f32[2048,64]{1,0:T(8,128)S(1)} all-gather(f32[32,64]{1,0:T(8,128)S(1)} %reshape.100), channel_id=1, replica_groups=mesh['coh'=4,'lat'=4,'lon'=16] {'lat','lon'}, dimensions={0}, use_global_device_ids=true | all-gather | bytes 532480 | tf_op jit(solution)/shard_map/all_gather | solution.py:98
  70.2 1.3 dynamic-slice
  72.1 0.8 convert_dynamic-update-slice_fusion
  72.9 109.3 %all-reduce = f32[2048]{0:T(1024)S(1)} all-reduce(f32[2048]{0:T(1024)S(1)} %convert_dynamic-update-slice_fusion), channel_id=1, replica_groups=mesh['coh'=4,'lat'=4,'lon'=16] {'lat','lon'}, use_global_device_ids=true, to_apply=%add | all-reduce | flops 2048 | bytes 16384
  182.3 0.9 slice_dynamic-update-slice_fusion.3
  183.2 0.8 slice_dynamic-update-slice_fusion.2
  184.1 22.3 %collective-permute-start.2 = (f32[35,1,256]{2,1,0:T(1,128)S(1)}, f32[35,1,256]{2,1,0:T(1,128)S(1)}, u32[]{:S(2)}, u32[]{:S(2)}) collective-permute-start(f32[35,1,256]{2,1,0:T(1,128)S(1)} %get-tuple-element.17), channel_id=1, source_target_pairs={{16,0},{32,16},{48,32},{17,1},{33,17},{49,33},{18,2},{34,18},{50,3... | collective-permute-start | bytes 107528 | tf_op jit(solution)/shard_map/ppermute | solution.py:31
  206.4 1.9 collective-permute-start.1
  208.8 3.4 collective-permute-done.1
  212.6 1.9 fusion.82
  214.5 1.9 copy.35
  216.3 1.3 collective-permute-start.3
  217.6 1.8 copy.36
  219.4 1.5 collective-permute-start.4
  221.0 1.6 slice.258
  222.7 3.9 %broadcast_in_dim.18 = f32[32,4,16,8,32]{4,3,2,1,0:T(8,128)} broadcast(f32[32,4,8]{2,1,0:T(4,128)S(1)} %copy.41), dimensions={0,1,3} | broadcast | bytes 2101248 | tf_op jit(solution)/shard_map/broadcast_in_dim | solution.py:164
  226.6 7.0 %reshape.102 = f32[32,64,256]{2,1,0:T(8,128)} reshape(f32[32,4,16,8,32]{4,3,2,1,0:T(8,128)} %broadcast_in_dim.18) | data formatting | bytes 4194304 | tf_op jit(solution)/shard_map/reshape | solution.py:172
  234.2 1.6 copy.37
  235.8 1.6 copy.38
  237.4 1.0 fusion.73
  240.7 1.2 slice_multiply_fusion.7
  242.0 13.6 %fusion.4 = f32[32,64,256]{2,1,0:T(8,128)S(1)} fusion(f32[32,64,256]{2,1,0:T(8,128)} %reshape.102, f32[35,66,1]{2,1,0:T(8,128)} %copy.37, f32[35,1,256]{2,1,0:T(1,128)} %copy-done.12, f32[35,64,256]{2,1,0:T(8,128)} %copy-done, f32[35,1,256]{2,1,0:T(1,128)} %copy-done.14, f32[32,66,258]{2,1,0:T(8,128)S(1)} %add_divide_fusion.1, f32[35,66,1]{2,1,0:T(8,128)} %copy.38, ...), kind=kLoop, calls=%fused_computation.11 | loop fusion | flops 25165824 | bytes 19554992 | tf_op jit(solution)/shard_map/add | solution.py:168
  255.6 1.4 collective-permute-start.5
  257.0 1.8 fusion.85
  258.8 4.0 %collective-permute-done.5 = f32[64,256]{1,0:T(8,128)S(1)} collective-permute-done((f32[64,256]{1,0:T(8,128)S(1)}, f32[64,256]{1,0:T(8,128)S(1)}, u32[]{:S(2)}, u32[]{:S(2)}) %collective-permute-start.5) | collective-permute-done | bytes 65568 | tf_op jit(solution)/shard_map/ppermute | solution.py:20
  262.9 1.9 collective-permute-start.7
  264.8 3.9 %collective-permute-start.6 = (f32[35,1,256]{2,1,0:T(1,128)S(1)}, f32[35,1,256]{2,1,0:T(1,128)S(1)}, u32[]{:S(2)}, u32[]{:S(2)}) collective-permute-start(f32[35,1,256]{2,1,0:T(1,128)S(1)} %get-tuple-element.14), channel_id=1, source_target_pairs={{0,16},{16,32},{32,48},{1,17},{17,33},{33,49},{2,18},{18,34},{34,5... | collective-permute-start | bytes 107528 | tf_op jit(solution)/shard_map/ppermute | solution.py:30
  268.9 3.9 %broadcast_in_dim.20 = f32[32,4,16,8,32]{4,3,2,1,0:T(8,128)} broadcast(f32[32,4,8]{2,1,0:T(4,128)S(1)} %copy.48), dimensions={0,1,3} | broadcast | bytes 2101248 | tf_op jit(solution)/shard_map/broadcast_in_dim | solution.py:164
  272.8 7.0 %reshape.104 = f32[32,64,256]{2,1,0:T(8,128)} reshape(f32[32,4,16,8,32]{4,3,2,1,0:T(8,128)} %broadcast_in_dim.20) | data formatting | bytes 4194304 | tf_op jit(solution)/shard_map/reshape | solution.py:172
  280.2 1.9 fusion.81
  282.1 1.8 copy.42
  283.8 1.6 collective-permute-start.8
  285.4 1.8 copy.43
  287.2 1.5 collective-permute-start.9
  288.8 1.5 broadcast_select_fusion
  290.3 1.6 copy.44
  291.9 1.6 copy.45
  293.5 1.0 fusion.71
  295.2 0.8 fusion.76
  296.8 37.3 %all-reduce.5.cloned.1.call-done = f32[64,256]{1,0:T(8,128)} async-done(((f32[64,256]{1,0:T(8,128)}), f32[64,256]{1,0:T(8,128)}) %all-reduce.5.cloned.1.call-update) | async-done | bytes 65552 | tf_op jit(solution)/shard_map/psum | solution.py:14
  334.1 1.9 multiply_add_fusion
  336.1 14.3 %fusion.6 = f32[32,64,256]{2,1,0:T(8,128)} fusion(f32[32,64,256]{2,1,0:T(8,128)} %reshape.104, f32[35,66,1]{2,1,0:T(8,128)} %copy.44, f32[35,1,256]{2,1,0:T(1,128)} %copy-done.11, f32[35,64,256]{2,1,0:T(8,128)} %copy-done.1, f32[35,1,256]{2,1,0:T(1,128)} %copy-done.13, f32[32,66,258]{2,1,0:T(8,128)S(1)} %add_divide_fusion, f32[35,66,1]{2,1,0:T(8,128)} %copy.45, ...), kind=kLoop, calls=%fused_computation.13 | loop fusion | flops 25165824 | bytes 19554992 | tf_op jit(solution)/shard_map/add | solution.py:168
  (105 shorter events, 7.5 us)
Async XLA Ops:
  7.2 233.5 %all-reduce.7.cloned.1.call-start = ((), (), s32[]{:S(2)}) async-start(), calls=%async_computation.1 | async-start | bytes 393216 | tf_op jit(solution)/shard_map/psum | solution.py:14
  8.7 3.7 %copy-start.8 = (f32[32,64,256]{2,1,0:T(8,128)}, f32[32,64,256]{2,1,0:T(8,128)S(1)}, u32[]{:S(2)}) copy-start(f32[32,64,256]{2,1,0:T(8,128)S(1)} %convert_element_type.33) | copy-start | bytes 6291460
  8.7 173.6 %collective-permute-start = (f32[64,256]{1,0:T(8,128)S(1)}, f32[64,256]{1,0:T(8,128)S(1)}, u32[]{:S(2)}, u32[]{:S(2)}) collective-permute-start(f32[64,256]{1,0:T(8,128)S(1)} %slice_bitcast_fusion.5), channel_id=1, source_target_pairs={{64,0},{128,64},{192,128},{65,1},{129,65},{193,129},{66,2},{130,66... | collective-permute-start | bytes 196616 | tf_op jit(solution)/shard_map/ppermute | solution.py:20
  10.7 1.7 copy-start.28
  12.4 4.5 %copy-start.20 = (f32[32]{0:T(128)}, f32[32]{0:T(128)S(1)}, u32[]{:S(2)}) copy-start(f32[32]{0:T(128)S(1)} %multiply_multiply_fusion.4) | copy-start | bytes 388
  15.0 1.9 copy-start.27
  15.0 2.0 copy-start.19
  15.0 319.1 %all-reduce.5.cloned.1.call-start = ((), (), s32[]{:S(2)}) async-start(), calls=%async_computation | async-start | bytes 131072 | tf_op jit(solution)/shard_map/psum | solution.py:14
  15.1 168.9 %copy-start.9 = (s32[64,256]{1,0:T(8,128)S(1)}, s32[64,256]{1,0:T(8,128)}, u32[]{:S(2)}) copy-start(s32[64,256]{1,0:T(8,128)} %param.22) | copy-start | bytes 196612
  182.3 24.1 %copy-start.15 = (f32[64,256]{1,0:T(8,128)}, f32[64,256]{1,0:T(8,128)S(1)}, u32[]{:S(2)}) copy-start(f32[64,256]{1,0:T(8,128)S(1)} %collective-permute-done) | copy-start | bytes 196612
  184.0 54.4 %copy-start = (f32[35,64,256]{2,1,0:T(8,128)}, f32[35,64,256]{2,1,0:T(8,128)S(1)}, u32[]{:S(2)}) copy-start(f32[35,64,256]{2,1,0:T(8,128)S(1)} %bitcast_dynamic-update-slice_fusion.1) | copy-start | bytes 6881284
  184.1 24.7 %collective-permute-start.2 = (f32[35,1,256]{2,1,0:T(1,128)S(1)}, f32[35,1,256]{2,1,0:T(1,128)S(1)}, u32[]{:S(2)}, u32[]{:S(2)}) collective-permute-start(f32[35,1,256]{2,1,0:T(1,128)S(1)} %get-tuple-element.17), channel_id=1, source_target_pairs={{16,0},{32,16},{48,32},{17,1},{33,17},{49,33},{18,2},{34,18},{50,3... | collective-permute-start | bytes 107528 | tf_op jit(solution)/shard_map/ppermute | solution.py:31
  206.4 5.8 %collective-permute-start.1 = (f32[35,1,256]{2,1,0:T(1,128)S(1)}, f32[35,1,256]{2,1,0:T(1,128)S(1)}, u32[]{:S(2)}, u32[]{:S(2)}) collective-permute-start(f32[35,1,256]{2,1,0:T(1,128)S(1)} %get-tuple-element.16), channel_id=1, source_target_pairs={{0,16},{16,32},{32,48},{1,17},{17,33},{33,49},{2,18},{18,34},{34,5... | collective-permute-start | bytes 107528 | tf_op jit(solution)/shard_map/ppermute | solution.py:30
  208.8 29.6 %copy-start.12 = (f32[35,1,256]{2,1,0:T(1,128)}, f32[35,1,256]{2,1,0:T(1,128)S(1)}, u32[]{:S(2)}) copy-start(f32[35,1,256]{2,1,0:T(1,128)S(1)} %collective-permute-done.2) | copy-start | bytes 107524
  212.2 26.2 %copy-start.14 = (f32[35,1,256]{2,1,0:T(1,128)}, f32[35,1,256]{2,1,0:T(1,128)S(1)}, u32[]{:S(2)}) copy-start(f32[35,1,256]{2,1,0:T(1,128)S(1)} %collective-permute-done.1) | copy-start | bytes 107524
  214.5 6.5 %copy-start.6 = (bf16[32,64,256]{2,1,0:T(8,128)(2,1)S(1)}, bf16[32,64,256]{2,1,0:T(8,128)(2,1)}, u32[]{:S(2)}) copy-start(bf16[32,64,256]{2,1,0:T(8,128)(2,1)} %param.19) | copy-start | bytes 3145732
  216.3 17.9 %collective-permute-start.3 = (f32[35,66,1]{1,2,0:T(1,128)S(1)}, f32[35,66,1]{1,2,0:T(1,128)S(1)}, u32[]{:S(2)}, u32[]{:S(2)}) collective-permute-start(f32[35,66,1]{1,2,0:T(1,128)S(1)} %copy.35), channel_id=1, source_target_pairs={{0,1},{1,2},{2,3},{3,4},{4,5},{5,6},{6,7},{7,8},{8,9},{9,10},{10,1... | collective-permute-start | bytes 27728 | tf_op jit(solution)/shard_map/ppermute | solution.py:30
  219.4 16.4 %collective-permute-start.4 = (f32[35,66,1]{1,2,0:T(1,128)S(1)}, f32[35,66,1]{1,2,0:T(1,128)S(1)}, u32[]{:S(2)}, u32[]{:S(2)}) collective-permute-start(f32[35,66,1]{1,2,0:T(1,128)S(1)} %copy.36), channel_id=1, source_target_pairs={{1,0},{2,1},{3,2},{4,3},{5,4},{6,5},{7,6},{8,7},{9,8},{10,9},{11,1... | collective-permute-start | bytes 27728 | tf_op jit(solution)/shard_map/ppermute | solution.py:31
  226.6 7.1 %copy-start.29 = (f32[32]{0:T(128)S(1)}, f32[32]{0:T(128)}, u32[]{:S(2)}) copy-start(f32[32]{0:T(128)} %param.25) | copy-start | bytes 388
  237.4 1.3 copy-start.3
  237.4 1.7 copy-start.5
  239.1 0.8 copy-start.25
  255.5 3.3 copy-start.7
  255.5 7.2 %copy-start.17 = (f32[2,64,256]{2,1,0:T(8,128)S(1)}, f32[2,64,256]{2,1,0:T(8,128)}, u32[]{:S(2)}) copy-start(f32[2,64,256]{2,1,0:T(8,128)} %param.20) | copy-start | bytes 393220
  255.5 7.2 %copy-start.18 = (f32[2,64,256]{2,1,0:T(8,128)S(1)}, f32[2,64,256]{2,1,0:T(8,128)}, u32[]{:S(2)}) copy-start(f32[2,64,256]{2,1,0:T(8,128)} %param.21) | copy-start | bytes 393220
  255.6 7.3 %copy-start.10 = (s32[64,256]{1,0:T(8,128)S(1)}, s32[64,256]{1,0:T(8,128)}, u32[]{:S(2)}) copy-start(s32[64,256]{1,0:T(8,128)} %param.22) | copy-start | bytes 196612
  255.6 7.2 %collective-permute-start.5 = (f32[64,256]{1,0:T(8,128)S(1)}, f32[64,256]{1,0:T(8,128)S(1)}, u32[]{:S(2)}, u32[]{:S(2)}) collective-permute-start(f32[64,256]{1,0:T(8,128)S(1)} %slice_bitcast_fusion.3), channel_id=1, source_target_pairs={{64,0},{128,64},{192,128},{65,1},{129,65},{193,129},{66,2},{130,66... | collective-permute-start | bytes 196616 | tf_op jit(solution)/shard_map/ppermute | solution.py:20
  262.8 6.0 %copy-start.16 = (f32[64,256]{1,0:T(8,128)}, f32[64,256]{1,0:T(8,128)S(1)}, u32[]{:S(2)}) copy-start(f32[64,256]{1,0:T(8,128)S(1)} %collective-permute-done.5) | copy-start | bytes 196612
  262.8 31.7 %copy-start.1 = (f32[35,64,256]{2,1,0:T(8,128)}, f32[35,64,256]{2,1,0:T(8,128)S(1)}, u32[]{:S(2)}) copy-start(f32[35,64,256]{2,1,0:T(8,128)S(1)} %bitcast_dynamic-update-slice_fusion) | copy-start | bytes 6881284
  262.9 16.9 %collective-permute-start.7 = (f32[35,1,256]{2,1,0:T(1,128)S(1)}, f32[35,1,256]{2,1,0:T(1,128)S(1)}, u32[]{:S(2)}, u32[]{:S(2)}) collective-permute-start(f32[35,1,256]{2,1,0:T(1,128)S(1)} %get-tuple-element.15), channel_id=1, source_target_pairs={{16,0},{32,16},{48,32},{17,1},{33,17},{49,33},{18,2},{34,18},{50,3... | collective-permute-start | bytes 107528 | tf_op jit(solution)/shard_map/ppermute | solution.py:31
  264.8 15.0 %collective-permute-start.6 = (f32[35,1,256]{2,1,0:T(1,128)S(1)}, f32[35,1,256]{2,1,0:T(1,128)S(1)}, u32[]{:S(2)}, u32[]{:S(2)}) collective-permute-start(f32[35,1,256]{2,1,0:T(1,128)S(1)} %get-tuple-element.14), channel_id=1, source_target_pairs={{0,16},{16,32},{32,48},{1,17},{17,33},{33,49},{2,18},{18,34},{34,5... | collective-permute-start | bytes 107528 | tf_op jit(solution)/shard_map/ppermute | solution.py:30
  279.8 14.7 %copy-start.11 = (f32[35,1,256]{2,1,0:T(1,128)}, f32[35,1,256]{2,1,0:T(1,128)S(1)}, u32[]{:S(2)}) copy-start(f32[35,1,256]{2,1,0:T(1,128)S(1)} %collective-permute-done.7) | copy-start | bytes 107524
  279.8 14.7 %copy-start.13 = (f32[35,1,256]{2,1,0:T(1,128)}, f32[35,1,256]{2,1,0:T(1,128)S(1)}, u32[]{:S(2)}) copy-start(f32[35,1,256]{2,1,0:T(1,128)S(1)} %collective-permute-done.6) | copy-start | bytes 107524
  283.8 6.4 %collective-permute-start.8 = (f32[35,66,1]{1,2,0:T(1,128)S(1)}, f32[35,66,1]{1,2,0:T(1,128)S(1)}, u32[]{:S(2)}, u32[]{:S(2)}) collective-permute-start(f32[35,66,1]{1,2,0:T(1,128)S(1)} %copy.42), channel_id=1, source_target_pairs={{0,1},{1,2},{2,3},{3,4},{4,5},{5,6},{6,7},{7,8},{8,9},{9,10},{10,1... | collective-permute-start | bytes 27728 | tf_op jit(solution)/shard_map/ppermute | solution.py:30
  287.2 4.6 %collective-permute-start.9 = (f32[35,66,1]{1,2,0:T(1,128)S(1)}, f32[35,66,1]{1,2,0:T(1,128)S(1)}, u32[]{:S(2)}, u32[]{:S(2)}) collective-permute-start(f32[35,66,1]{1,2,0:T(1,128)S(1)} %copy.43), channel_id=1, source_target_pairs={{1,0},{2,1},{3,2},{4,3},{5,4},{6,5},{7,6},{8,7},{9,8},{10,9},{11,1... | collective-permute-start | bytes 27728 | tf_op jit(solution)/shard_map/ppermute | solution.py:31
  293.5 1.3 copy-start.2
  293.5 1.7 copy-start.4
  295.2 0.8 copy-start.26
  296.0 40.0 %copy-start.21 = (f32[32]{0:T(128)S(1)}, f32[32]{0:T(128)}, u32[]{:S(2)}) copy-start(f32[32]{0:T(128)} %copy-done.20) | copy-start | bytes 388
  296.0 40.0 %copy-start.22 = (f32[32]{0:T(128)S(1)}, f32[32]{0:T(128)}, u32[]{:S(2)}) copy-start(f32[32]{0:T(128)} %param.28) | copy-start | bytes 388
  296.0 40.0 %copy-start.23 = (f32[32]{0:T(128)S(1)}, f32[32]{0:T(128)}, u32[]{:S(2)}) copy-start(f32[32]{0:T(128)} %param.27) | copy-start | bytes 388
  296.0 40.0 %copy-start.24 = (f32[32]{0:T(128)S(1)}, f32[32]{0:T(128)}, u32[]{:S(2)}) copy-start(f32[32]{0:T(128)} %param.26) | copy-start | bytes 388
Sparse Core Ops, SparseCore 0:
  15.2 50.9 all-reduce.6
  290.4 43.6 all-reduce.4
where the time goes:
time: 358 us; the launch traced here: 357 us
  blocking collectives  162 us (45%)
  local copies, waits for them, and re-layouts  51 us (14%)
  waiting for transfers between devices  44.8 us (13%)
  other arithmetic  42.6 us (12%)
  starting transfers between devices  38.8 us (11%)
  between operations  15.3 us (4%)
    unnamed x1, blocking collectives  109 us
    all_gather x1, blocking collectives, shards(): lax.all_gather(masked, ('lat', 'lon'), axis=0, tiled=True)  53 us
    psum x2, waiting for transfers between devices, from_root(): return lax.psum(kept, axis)  37.3 us
    add x2, other arithmetic, shards(): survive * after_move + recruit_term[None] * maturity[:, None, None]  27.9 us
    ppermute x4, starting transfers between devices, with_halo(): after = lax.ppermute(first, axis, down)  27.2 us
    reshape x2, local copies, waits for them, and re-layouts, shards(): spread.reshape(ages_here, rows_y, rows_x)  14.1 us
    ppermute x4, starting transfers between devices, with_halo(): before = lax.ppermute(last, axis, up)  8.77 us
    broadcast_in_dim x2, local copies, waits for them, and re-layouts, shards(): jnp.broadcast_to(block_grid[:, :, None, :, None], (ages_here, blocks_y, B...  7.82 us
  transfers between devices with their start and end apart: 12, of which 3 were waited for; matrix products, arithmetic and copies ran while one was open for 16% of the time, Pallas kernels for 0%

commit v1 on v0

--- a/solution.py
+++ b/solution.py
@@ -7,6 +7,14 @@
 BX = 32
 thermal_tolerance_spread = 4.0
 highest = lax.Precision.HIGHEST
+
+
+def gather_from_all(array, axis, dim):
+    devices = lax.axis_size(axis)
+    repeats = [devices if d == dim else 1 for d in range(array.ndim)]
+    return lax.all_to_all(
+        jnp.tile(array, repeats), axis, split_axis=dim, concat_axis=dim, tiled=True
+    )
 
 
 def from_root(value, axis, source):
@@ -95,7 +103,7 @@
         (lat_pos * lon_count + lon_pos) * nblocks,
         nblocks,
         (
-            lax.all_gather(masked, ("lat", "lon"), axis=0, tiled=True),
+            gather_from_all(masked, ("lat", "lon"), 0),
             lax.all_gather(place_id, ("lat", "lon"), axis=0, tiled=True),
         ),
     )

time: 358 us -> 334 us (0.933)
  blocking collectives: 162 us -> 110 us
  starting transfers between devices: 38.8 us -> 53.8 us
  local copies, waits for them, and re-layouts: 51 us -> 58.3 us
  other arithmetic: 42.6 us -> 46.3 us
    all_gather x1 -> x0, blocking collectives: 53 us -> none  [shards(): lax.all_gather(masked, ('lat', 'lon'), axis=0, tiled=True)]
    all_to_all x0 -> x1, starting transfers between devices: none -> 12.3 us  [gather_from_all(): lax.all_to_all(jnp.tile(array, repeats), axis, split_axis=dim, concat_axi...]
    all_to_all x0 -> x1, other arithmetic: none -> 3.73 us  [gather_from_all(): lax.all_to_all(jnp.tile(array, repeats), axis, split_axis=dim, concat_axi...]
    unnamed x69 -> x73, local copies, waits for them, and re-layouts: 6.18 us -> 9.38 us
  transfers between devices with their start and end apart: 12 -> 13, of which waited for: 3 -> 4; matrix products, arithmetic and copies ran while one was open for 16% -> 14% of each run, Pallas kernels for 0% -> 0%
where the time goes in v1:
time: 334 us; the launch traced here: 333 us
  blocking collectives  110 us (33%)
  local copies, waits for them, and re-layouts  58.3 us (17%)
  starting transfers between devices  53.8 us (16%)
  other arithmetic  46.3 us (14%)
  waiting for transfers between devices  45.2 us (14%)
  between operations  15.4 us (5%)
  matrix products  3.64 us (1%)
    unnamed x1, blocking collectives  110 us
    psum x2, waiting for transfers between devices, from_root(): return lax.psum(kept, axis)  36 us
    ppermute x4, starting transfers between devices, with_halo(): after = lax.ppermute(first, axis, down)  30.7 us
    add x2, other arithmetic, shards(): survive * after_move + recruit_term[None] * maturity[:, None, None]  27.6 us
    reshape x2, local copies, waits for them, and re-layouts, shards(): spread.reshape(ages_here, rows_y, rows_x)  14.1 us
    all_to_all x1, starting transfers between devices, gather_from_all(): lax.all_to_all(jnp.tile(array, repeats), axis, split_axis=dim, concat_axi...  12.3 us
    unnamed x73, local copies, waits for them, and re-layouts  9.38 us
    broadcast_in_dim x2, local copies, waits for them, and re-layouts, shards(): jnp.broadcast_to(block_grid[:, :, None, :, None], (ages_here, blocks_y, B...  8.65 us
  transfers between devices with their start and end apart: 13, of which 4 were waited for; matrix products, arithmetic and copies ran while one was open for 14% of the time, Pallas kernels for 0%

profile of v1, /device:TPU:2, one launch (start us, length us, event | category | flops | bytes accessed | tf_op | source)
XLA Modules:
  0.0 332.7 jit_solution(3960462121663116637)
XLA Ops:
  9.0 1.5 reshape.117
  10.5 12.3 %all-to-all-start = ((f32[64,1,2048]{2,1,0:T(1,128)}), f32[64,1,2048]{2,1,0:T(1,128)}, u32[]{:S(2)}, u32[]{:S(2)}) async-start(f32[64,1,2048]{2,1,0:T(1,128)} %reshape.117), calls=%async_computation | async-start | bytes 1048576 | tf_op jit(solution)/shard_map/all_to_all | solution.py:15
  23.2 1.3 collective-permute-start
  25.2 1.7 slice_bitcast_fusion.1
  26.9 1.0 fusion.63
  27.9 1.0 fusion.65
  29.6 1.7 constant_dynamic-update-slice_fusion.1
  34.4 2.4 collective-permute-start.2
  36.9 3.4 %collective-permute-start.1 = (f32[35,1,256]{2,1,0:T(1,128)S(1)}, f32[35,1,256]{2,1,0:T(1,128)S(1)}, u32[]{:S(2)}, u32[]{:S(2)}) collective-permute-start(f32[35,1,256]{2,1,0:T(1,128)S(1)} %get-tuple-element.16), channel_id=1, source_target_pairs={{0,16},{16,32},{32,48},{1,17},{17,33},{33,49},{2,18},{18,34},{34,5... | collective-permute-start | bytes 107528 | tf_op jit(solution)/shard_map/ppermute | solution.py:38
  41.1 1.6 collective-permute-done.1
  43.1 1.9 fusion.82
  45.0 1.8 copy.35
  46.7 1.3 collective-permute-start.3
  48.1 1.8 copy.36
  49.8 1.4 collective-permute-start.4
  51.3 1.6 slice.258
  53.5 110.1 %all-reduce = f32[2048]{0:T(1024)S(1)} all-reduce(f32[2048]{0:T(1024)S(1)} %convert_dynamic-update-slice_fusion), channel_id=1, replica_groups=mesh['coh'=4,'lat'=4,'lon'=16] {'lat','lon'}, use_global_device_ids=true, to_apply=%add | all-reduce | flops 2048 | bytes 16384
  163.6 1.6 copy.37
  165.2 1.6 copy.38
  166.8 1.0 fusion.73
  170.1 1.9 slice_multiply_fusion.7
  172.6 3.7 %reduce = f32[64,2048]{1,0:T(8,128)} reduce(f32[64,1,2048]{2,1,0:T(1,128)} %all-to-all-done, f32[]{:T(128)} %broadcast.96), dimensions={1}, to_apply=%all_to_all.6.reduce_sub_computation | reduce | bytes 1048580 | tf_op jit(solution)/shard_map/all_to_all | solution.py:15
  176.3 2.4 reshape.118
  178.7 1.7 fusion.67
  181.1 1.4 copy.41
  182.6 4.7 %broadcast_in_dim.18 = f32[32,4,16,8,32]{4,3,2,1,0:T(8,128)} broadcast(f32[32,4,8]{2,1,0:T(4,128)} %copy.41), dimensions={0,1,3} | broadcast | bytes 2101248 | tf_op jit(solution)/shard_map/broadcast_in_dim | solution.py:172
  187.3 7.0 %reshape.105 = f32[32,64,256]{2,1,0:T(8,128)} reshape(f32[32,4,16,8,32]{4,3,2,1,0:T(8,128)} %broadcast_in_dim.18) | data formatting | bytes 4194304 | tf_op jit(solution)/shard_map/reshape | solution.py:180
  194.3 13.3 %fusion.4 = f32[32,64,256]{2,1,0:T(8,128)S(1)} fusion(f32[32,64,256]{2,1,0:T(8,128)} %reshape.105, f32[35,66,1]{2,1,0:T(8,128)} %copy.37, f32[35,1,256]{2,1,0:T(1,128)} %copy-done.11, f32[35,64,256]{2,1,0:T(8,128)} %copy-done, f32[35,1,256]{2,1,0:T(1,128)} %copy-done.12, f32[32,66,258]{2,1,0:T(8,128)S(1)} %add_divide_fusion.1, f32[35,66,1]{2,1,0:T(8,128)} %copy.38, ...), kind=kLoop, calls=%fused_computation.11 | loop fusion | flops 25165824 | bytes 19554992 | tf_op jit(solution)/shard_map/add | solution.py:176
  207.7 1.4 collective-permute-start.5
  209.1 1.9 fusion.85
  211.0 3.6 %collective-permute-done.5 = f32[64,256]{1,0:T(8,128)S(1)} collective-permute-done((f32[64,256]{1,0:T(8,128)S(1)}, f32[64,256]{1,0:T(8,128)S(1)}, u32[]{:S(2)}, u32[]{:S(2)}) %collective-permute-start.5) | collective-permute-done | bytes 65568 | tf_op jit(solution)/shard_map/ppermute | solution.py:28
  214.8 25.3 %collective-permute-start.7 = (f32[35,1,256]{2,1,0:T(1,128)S(1)}, f32[35,1,256]{2,1,0:T(1,128)S(1)}, u32[]{:S(2)}, u32[]{:S(2)}) collective-permute-start(f32[35,1,256]{2,1,0:T(1,128)S(1)} %get-tuple-element.15), channel_id=1, source_target_pairs={{16,0},{32,16},{48,32},{17,1},{33,17},{49,33},{18,2},{34,18},{50,3... | collective-permute-start | bytes 107528 | tf_op jit(solution)/shard_map/ppermute | solution.py:39
  240.1 1.9 collective-permute-start.6
  242.0 3.9 %collective-permute-done.6 = f32[35,1,256]{2,1,0:T(1,128)S(1)} collective-permute-done((f32[35,1,256]{2,1,0:T(1,128)S(1)}, f32[35,1,256]{2,1,0:T(1,128)S(1)}, u32[]{:S(2)}, u32[]{:S(2)}) %collective-permute-start.6) | collective-permute-done | bytes 35872 | tf_op jit(solution)/shard_map/ppermute | solution.py:38
  246.3 1.9 fusion.81
  248.2 1.8 copy.42
  249.9 1.3 collective-permute-start.8
  251.2 1.8 copy.43
  253.0 1.5 collective-permute-start.9
  254.5 1.5 broadcast_select_fusion
  256.1 3.9 %broadcast_in_dim.20 = f32[32,4,16,8,32]{4,3,2,1,0:T(8,128)} broadcast(f32[32,4,8]{2,1,0:T(4,128)S(1)} %copy.48), dimensions={0,1,3} | broadcast | bytes 2101248 | tf_op jit(solution)/shard_map/broadcast_in_dim | solution.py:172
  260.0 7.0 %reshape.107 = f32[32,64,256]{2,1,0:T(8,128)} reshape(f32[32,4,16,8,32]{4,3,2,1,0:T(8,128)} %broadcast_in_dim.20) | data formatting | bytes 4194304 | tf_op jit(solution)/shard_map/reshape | solution.py:180
  267.1 1.6 copy.44
  268.7 1.6 copy.45
  270.3 1.0 fusion.71
  273.6 36.0 %all-reduce.5.cloned.1.call-done = f32[64,256]{1,0:T(8,128)} async-done(((f32[64,256]{1,0:T(8,128)}), f32[64,256]{1,0:T(8,128)}) %all-reduce.5.cloned.1.call-update) | async-done | bytes 65552 | tf_op jit(solution)/shard_map/psum | solution.py:22
  309.6 2.0 multiply_add_fusion
  311.6 14.3 %fusion.6 = f32[32,64,256]{2,1,0:T(8,128)} fusion(f32[32,64,256]{2,1,0:T(8,128)} %reshape.107, f32[35,66,1]{2,1,0:T(8,128)} %copy.44, f32[35,1,256]{2,1,0:T(1,128)} %copy-done.13, f32[35,64,256]{2,1,0:T(8,128)} %copy-done.1, f32[35,1,256]{2,1,0:T(1,128)} %copy-done.14, f32[32,66,258]{2,1,0:T(8,128)S(1)} %add_divide_fusion, f32[35,66,1]{2,1,0:T(8,128)} %copy.45, ...), kind=kLoop, calls=%fused_computation.13 | loop fusion | flops 25165824 | bytes 19554992 | tf_op jit(solution)/shard_map/add | solution.py:176
  (113 shorter events, 13.8 us)
Async XLA Ops:
  7.2 15.7 %copy-start.6 = (bf16[32,64,256]{2,1,0:T(8,128)(2,1)S(1)}, bf16[32,64,256]{2,1,0:T(8,128)(2,1)}, u32[]{:S(2)}) copy-start(bf16[32,64,256]{2,1,0:T(8,128)(2,1)} %param.19) | copy-start | bytes 3145732
  10.5 14.0 %copy-start.28 = (f32[32]{0:T(128)S(1)}, f32[32]{0:T(128)}, u32[]{:S(2)}) copy-start(f32[32]{0:T(128)} %param.30) | copy-start | bytes 388
  10.5 161.5 %all-to-all-start = ((f32[64,1,2048]{2,1,0:T(1,128)}), f32[64,1,2048]{2,1,0:T(1,128)}, u32[]{:S(2)}, u32[]{:S(2)}) async-start(f32[64,1,2048]{2,1,0:T(1,128)} %reshape.117), calls=%async_computation | async-start | bytes 1048576 | tf_op jit(solution)/shard_map/all_to_all | solution.py:15
  22.9 147.2 %all-reduce.7.cloned.1.call-start = ((), (), s32[]{:S(2)}) async-start(), calls=%async_computation.2 | async-start | bytes 393216 | tf_op jit(solution)/shard_map/psum | solution.py:22
  23.2 3.7 %copy-start.8 = (f32[32,64,256]{2,1,0:T(8,128)}, f32[32,64,256]{2,1,0:T(8,128)S(1)}, u32[]{:S(2)}) copy-start(f32[32,64,256]{2,1,0:T(8,128)S(1)} %convert_element_type.33) | copy-start | bytes 6291460
  23.2 9.4 %collective-permute-start = (f32[64,256]{1,0:T(8,128)S(1)}, f32[64,256]{1,0:T(8,128)S(1)}, u32[]{:S(2)}, u32[]{:S(2)}) collective-permute-start(f32[64,256]{1,0:T(8,128)S(1)} %slice_bitcast_fusion.5), channel_id=1, source_target_pairs={{64,0},{128,64},{192,128},{65,1},{129,65},{193,129},{66,2},{130,66... | collective-permute-start | bytes 196616 | tf_op jit(solution)/shard_map/ppermute | solution.py:28
  24.5 3.3 copy-start.19
  29.5 1.9 copy-start.30
  29.5 4.8 %copy-start.9 = (s32[64,256]{1,0:T(8,128)S(1)}, s32[64,256]{1,0:T(8,128)}, u32[]{:S(2)}) copy-start(s32[64,256]{1,0:T(8,128)} %param.22) | copy-start | bytes 196612
  29.5 10.8 %copy-start.26 = (s32[32]{0:T(128)S(1)}, s32[32]{0:T(128)}, u32[]{:S(2)}) copy-start(s32[32]{0:T(128)} %param.34) | copy-start | bytes 388
  29.6 10.8 %copy-start.27 = (s32[32,1]{0,1:T(1,128)S(1)}, s32[32,1]{0,1:T(1,128)}, u32[]{:S(2)}) copy-start(s32[32,1]{0,1:T(1,128)} %param.32) | copy-start | bytes 388
  29.6 280.0 %all-reduce.5.cloned.1.call-start = ((), (), s32[]{:S(2)}) async-start(), calls=%async_computation.1 | async-start | bytes 131072 | tf_op jit(solution)/shard_map/psum | solution.py:22
  32.6 4.3 %copy-start.15 = (f32[64,256]{1,0:T(8,128)}, f32[64,256]{1,0:T(8,128)S(1)}, u32[]{:S(2)}) copy-start(f32[64,256]{1,0:T(8,128)S(1)} %collective-permute-done) | copy-start | bytes 196612
  34.4 133.5 %copy-start = (f32[35,64,256]{2,1,0:T(8,128)}, f32[35,64,256]{2,1,0:T(8,128)S(1)}, u32[]{:S(2)}) copy-start(f32[35,64,256]{2,1,0:T(8,128)S(1)} %bitcast_dynamic-update-slice_fusion.1) | copy-start | bytes 6881284
  34.4 6.7 %collective-permute-start.2 = (f32[35,1,256]{2,1,0:T(1,128)S(1)}, f32[35,1,256]{2,1,0:T(1,128)S(1)}, u32[]{:S(2)}, u32[]{:S(2)}) collective-permute-start(f32[35,1,256]{2,1,0:T(1,128)S(1)} %get-tuple-element.17), channel_id=1, source_target_pairs={{16,0},{32,16},{48,32},{17,1},{33,17},{49,33},{18,2},{34,18},{50,3... | collective-permute-start | bytes 107528 | tf_op jit(solution)/shard_map/ppermute | solution.py:39
  36.9 5.8 %collective-permute-start.1 = (f32[35,1,256]{2,1,0:T(1,128)S(1)}, f32[35,1,256]{2,1,0:T(1,128)S(1)}, u32[]{:S(2)}, u32[]{:S(2)}) collective-permute-start(f32[35,1,256]{2,1,0:T(1,128)S(1)} %get-tuple-element.16), channel_id=1, source_target_pairs={{0,16},{16,32},{32,48},{1,17},{17,33},{33,49},{2,18},{18,34},{34,5... | collective-permute-start | bytes 107528 | tf_op jit(solution)/shard_map/ppermute | solution.py:38
  41.1 126.7 %copy-start.11 = (f32[35,1,256]{2,1,0:T(1,128)}, f32[35,1,256]{2,1,0:T(1,128)S(1)}, u32[]{:S(2)}) copy-start(f32[35,1,256]{2,1,0:T(1,128)S(1)} %collective-permute-done.2) | copy-start | bytes 107524
  42.7 125.1 %copy-start.12 = (f32[35,1,256]{2,1,0:T(1,128)}, f32[35,1,256]{2,1,0:T(1,128)S(1)}, u32[]{:S(2)}) copy-start(f32[35,1,256]{2,1,0:T(1,128)S(1)} %collective-permute-done.1) | copy-start | bytes 107524
  46.7 116.8 %collective-permute-start.3 = (f32[35,66,1]{1,2,0:T(1,128)S(1)}, f32[35,66,1]{1,2,0:T(1,128)S(1)}, u32[]{:S(2)}, u32[]{:S(2)}) collective-permute-start(f32[35,66,1]{1,2,0:T(1,128)S(1)} %copy.35), channel_id=1, source_target_pairs={{0,1},{1,2},{2,3},{3,4},{4,5},{5,6},{6,7},{7,8},{8,9},{9,10},{10,1... | collective-permute-start | bytes 27728 | tf_op jit(solution)/shard_map/ppermute | solution.py:38
  49.8 3.1 copy-start.29
  49.8 115.3 %collective-permute-start.4 = (f32[35,66,1]{1,2,0:T(1,128)S(1)}, f32[35,66,1]{1,2,0:T(1,128)S(1)}, u32[]{:S(2)}, u32[]{:S(2)}) collective-permute-start(f32[35,66,1]{1,2,0:T(1,128)S(1)} %copy.36), channel_id=1, source_target_pairs={{1,0},{2,1},{3,2},{4,3},{5,4},{6,5},{7,6},{8,7},{9,8},{10,9},{11,1... | collective-permute-start | bytes 27728 | tf_op jit(solution)/shard_map/ppermute | solution.py:39
  166.8 1.3 copy-start.2
  166.8 1.7 copy-start.3
  168.5 0.8 copy-start.24
  207.6 3.4 %copy-start.7 = (f32[32,64,256]{2,1,0:T(8,128)}, f32[32,64,256]{2,1,0:T(8,128)S(1)}, u32[]{:S(2)}) copy-start(f32[32,64,256]{2,1,0:T(8,128)S(1)} %fusion.4) | copy-start | bytes 6291460
  207.7 7.0 %copy-start.17 = (f32[2,64,256]{2,1,0:T(8,128)S(1)}, f32[2,64,256]{2,1,0:T(8,128)}, u32[]{:S(2)}) copy-start(f32[2,64,256]{2,1,0:T(8,128)} %param.20) | copy-start | bytes 393220
  207.7 7.0 %copy-start.18 = (f32[2,64,256]{2,1,0:T(8,128)S(1)}, f32[2,64,256]{2,1,0:T(8,128)}, u32[]{:S(2)}) copy-start(f32[2,64,256]{2,1,0:T(8,128)} %param.21) | copy-start | bytes 393220
  207.7 7.0 %copy-start.10 = (s32[64,256]{1,0:T(8,128)S(1)}, s32[64,256]{1,0:T(8,128)}, u32[]{:S(2)}) copy-start(s32[64,256]{1,0:T(8,128)} %param.22) | copy-start | bytes 196612
  207.7 6.9 %collective-permute-start.5 = (f32[64,256]{1,0:T(8,128)S(1)}, f32[64,256]{1,0:T(8,128)S(1)}, u32[]{:S(2)}, u32[]{:S(2)}) collective-permute-start(f32[64,256]{1,0:T(8,128)S(1)} %slice_bitcast_fusion.3), channel_id=1, source_target_pairs={{64,0},{128,64},{192,128},{65,1},{129,65},{193,129},{66,2},{130,66... | collective-permute-start | bytes 196616 | tf_op jit(solution)/shard_map/ppermute | solution.py:28
  214.6 31.6 %copy-start.16 = (f32[64,256]{1,0:T(8,128)}, f32[64,256]{1,0:T(8,128)S(1)}, u32[]{:S(2)}) copy-start(f32[64,256]{1,0:T(8,128)S(1)} %collective-permute-done.5) | copy-start | bytes 196612
  214.7 56.6 %copy-start.1 = (f32[35,64,256]{2,1,0:T(8,128)}, f32[35,64,256]{2,1,0:T(8,128)S(1)}, u32[]{:S(2)}) copy-start(f32[35,64,256]{2,1,0:T(8,128)S(1)} %bitcast_dynamic-update-slice_fusion) | copy-start | bytes 6881284
  214.8 27.2 %collective-permute-start.7 = (f32[35,1,256]{2,1,0:T(1,128)S(1)}, f32[35,1,256]{2,1,0:T(1,128)S(1)}, u32[]{:S(2)}, u32[]{:S(2)}) collective-permute-start(f32[35,1,256]{2,1,0:T(1,128)S(1)} %get-tuple-element.15), channel_id=1, source_target_pairs={{16,0},{32,16},{48,32},{17,1},{33,17},{49,33},{18,2},{34,18},{50,3... | collective-permute-start | bytes 107528 | tf_op jit(solution)/shard_map/ppermute | solution.py:39
  240.1 5.8 %collective-permute-start.6 = (f32[35,1,256]{2,1,0:T(1,128)S(1)}, f32[35,1,256]{2,1,0:T(1,128)S(1)}, u32[]{:S(2)}, u32[]{:S(2)}) collective-permute-start(f32[35,1,256]{2,1,0:T(1,128)S(1)} %get-tuple-element.14), channel_id=1, source_target_pairs={{0,16},{16,32},{32,48},{1,17},{17,33},{33,49},{2,18},{18,34},{34,5... | collective-permute-start | bytes 107528 | tf_op jit(solution)/shard_map/ppermute | solution.py:38
  242.0 29.3 %copy-start.13 = (f32[35,1,256]{2,1,0:T(1,128)}, f32[35,1,256]{2,1,0:T(1,128)S(1)}, u32[]{:S(2)}) copy-start(f32[35,1,256]{2,1,0:T(1,128)S(1)} %collective-permute-done.7) | copy-start | bytes 107524
  245.9 25.4 %copy-start.14 = (f32[35,1,256]{2,1,0:T(1,128)}, f32[35,1,256]{2,1,0:T(1,128)S(1)}, u32[]{:S(2)}) copy-start(f32[35,1,256]{2,1,0:T(1,128)S(1)} %collective-permute-done.6) | copy-start | bytes 107524
  249.9 17.2 %collective-permute-start.8 = (f32[35,66,1]{1,2,0:T(1,128)S(1)}, f32[35,66,1]{1,2,0:T(1,128)S(1)}, u32[]{:S(2)}, u32[]{:S(2)}) collective-permute-start(f32[35,66,1]{1,2,0:T(1,128)S(1)} %copy.42), channel_id=1, source_target_pairs={{0,1},{1,2},{2,3},{3,4},{4,5},{5,6},{6,7},{7,8},{8,9},{9,10},{10,1... | collective-permute-start | bytes 27728 | tf_op jit(solution)/shard_map/ppermute | solution.py:38
  253.0 15.7 %collective-permute-start.9 = (f32[35,66,1]{1,2,0:T(1,128)S(1)}, f32[35,66,1]{1,2,0:T(1,128)S(1)}, u32[]{:S(2)}, u32[]{:S(2)}) collective-permute-start(f32[35,66,1]{1,2,0:T(1,128)S(1)} %copy.43), channel_id=1, source_target_pairs={{1,0},{2,1},{3,2},{4,3},{5,4},{6,5},{7,6},{8,7},{9,8},{10,9},{11,1... | collective-permute-start | bytes 27728 | tf_op jit(solution)/shard_map/ppermute | solution.py:39
  270.3 1.3 copy-start.4
  270.3 1.7 copy-start.5
  272.0 0.8 copy-start.25
  272.8 38.8 %copy-start.20 = (f32[32]{0:T(128)S(1)}, f32[32]{0:T(128)}, u32[]{:S(2)}) copy-start(f32[32]{0:T(128)} %copy-done.19) | copy-start | bytes 388
  272.8 38.8 %copy-start.21 = (f32[32]{0:T(128)S(1)}, f32[32]{0:T(128)}, u32[]{:S(2)}) copy-start(f32[32]{0:T(128)} %param.28) | copy-start | bytes 388
  272.8 38.8 %copy-start.22 = (f32[32]{0:T(128)S(1)}, f32[32]{0:T(128)}, u32[]{:S(2)}) copy-start(f32[32]{0:T(128)} %param.27) | copy-start | bytes 388
  272.8 38.8 %copy-start.23 = (f32[32]{0:T(128)S(1)}, f32[32]{0:T(128)}, u32[]{:S(2)}) copy-start(f32[32]{0:T(128)} %param.26) | copy-start | bytes 388
Sparse Core Ops, SparseCore 0:
  29.6 49.2 all-reduce.6
  267.2 42.3 all-reduce.4
